TPU v7x, 128 devices: a whole 4x4x4 slice. The times are simulated.
128 devices in a mesh: fronts: 8 (over y, core), rows: 16 (over z, x).
Axes of the slice: x: 4, y: 4, z: 4, core: 2. Of those that a mesh axis runs over, the one named last changes fastest.
Arguments:
- lower_rhs: float32 [16, 16384, 512], P('fronts', 'rows'), may hold values from -6 to 6
- lower_vectors: float32 [16, 16384, 256], P('fronts', 'rows')
- lower_factors: float32 [16, 16, 256, 256], P('fronts', 'rows')
- merge_vectors: float32 [16, 16, 256, 256], P('fronts', 'rows')
- merge_factors: float32 [16, 16, 256, 256], P('fronts', 'rows')
- live_blocks: int32 [16], replicated, may hold values from 1 to 16, 128 in all
- parent_front: int32 [16, 1], replicated, may hold values from 0 to 7, as said below
- front_owner: int32 [8], replicated, may hold values from 0 to 7, as said below
- contrib_rows: int32 [16, 128], replicated, may hold values from 0 to 16383, as said below
- upper_rhs: float32 [8, 16384, 512], P('fronts', 'rows'), may hold values from -6 to 6
- upper_vectors: float32 [8, 16384, 256], P('fronts', 'rows')
- upper_factors: float32 [8, 16, 256, 256], P('fronts', 'rows')
- summit_vectors: float32 [8, 16, 256, 256], P('fronts', 'rows')
- summit_factors: float32 [8, 16, 256, 256], P('fronts', 'rows')
Outputs:
- lower_result: float32 [16, 16384, 512], P('fronts', 'rows')
- upper_result: float32 [8, 16384, 512], P('fronts', 'rows')
Inputs may be any that keep to these rules, and one draw needn't show every extreme that they name: `parent_front`: every parent front has between one and 4 children, and some parent has exactly 4. `front_owner`: each parent front has its own index of fronts. `contrib_rows`: row k of a child's contribution lands in its parent's row block k // 8; no two entries are equal.
All inputs are finite; a program needn't handle non-finite values.
Results may differ from a plain program's by a relative error of at most 0.0003.
Values sent between devices are 32-bit elements; how exact they have to be, the bound alone decides.
No kernel may reach another device: no remote copies, remote signals or barrier semaphores. Data moves between devices by JAX's collectives and lax.ppermute only.
A program may use at most 128 MiB of HBM per device.

v0:
```python
import jax
import jax.numpy as jnp
from jax import lax
from jax.sharding import PartitionSpec as P

NPIV = 128
EXACT = lax.Precision.HIGHEST


def partner(value, axis, bit):
    mask = 2**bit
    pairs = [(source, source ^ mask) for source in range(lax.axis_size(axis))]
    return lax.ppermute(value, axis, pairs)


def from_root(value, axis, source):
    kept = jnp.where(lax.axis_index(axis) == source, value, 0).astype(value.dtype)
    return lax.psum(kept, axis)


def wy_apply(values, vectors, factors):
    project = jnp.einsum("fri,frn->fin", vectors, values, precision=EXACT)
    scaled = jnp.einsum("fij,fin->fjn", factors, project, precision=EXACT)
    return values - jnp.einsum("fri,fin->frn", vectors, scaled, precision=EXACT)


def combine(lead, rest, vectors, factors):
    inner = lead + jnp.einsum("fij,fin->fjn", vectors, rest, precision=EXACT)
    weight = jnp.einsum("fij,fin->fjn", factors, inner, precision=EXACT)
    return (lead - weight, rest - jnp.einsum("fij,fjn->fin", vectors, weight, precision=EXACT))


def run_tree(tops, vectors, factors, live, place):
    levels = lax.axis_size("rows").bit_length() - 1
    for level in range(levels):
        step = 1 << level
        leads = (place % (2 * step) == 0) & (place + step < live)
        follows = (place % (2 * step) == step) & (place < live)
        lead_side = leads[:, None, None]
        follow_side = follows[:, None, None]
        other, other_vectors, other_factors = partner((tops, vectors, factors), "rows", level)
        lead_part = jnp.where(lead_side, tops, other)
        rest_part = jnp.where(lead_side, other, tops)
        node_vectors = jnp.where(lead_side, other_vectors, vectors)
        node_factors = jnp.where(lead_side, other_factors, factors)
        lead_new, rest_new = combine(lead_part, rest_part, node_vectors, node_factors)
        tops = jnp.where(lead_side, lead_new, jnp.where(follow_side, rest_new, tops))
    return tops


def per_device(
    lower_rhs,
    lower_vectors,
    lower_factors,
    merge_vectors,
    merge_factors,
    live_blocks,
    parent_front,
    front_owner,
    contrib_rows,
    upper_rhs,
    upper_vectors,
    upper_factors,
    summit_vectors,
    summit_factors,
):
    place = lax.axis_index("rows")
    column = lax.axis_index("fronts")
    blocks = lax.axis_size("rows")
    local_fronts = lower_rhs.shape[0]
    height = lower_rhs.shape[1]
    width = lower_factors.shape[-1]
    live = lax.dynamic_slice_in_dim(live_blocks, column * local_fronts, local_fronts)
    applied = wy_apply(lower_rhs, lower_vectors, lower_factors[:, 0])
    applied = jnp.where((place < live)[:, None, None], applied, lower_rhs)
    tops = run_tree(applied[:, :width], merge_vectors[:, 0], merge_factors[:, 0], live, place)
    keep = (jnp.arange(width) < NPIV)[None, :, None] | (place != 0)
    lower_result = jnp.concatenate([jnp.where(keep, tops, 0.0), applied[:, width:]], axis=1)
    contrib = tops[:, NPIV:]
    share = (width - NPIV) // blocks
    shared = from_root(contrib, "rows", 0)
    gathered = lax.all_gather(shared, "fronts", axis=0, tiled=True)
    front_portions = lax.dynamic_slice_in_dim(gathered, place * share, share, 1)
    parents = jnp.arange(front_owner.shape[0], dtype=jnp.int32)
    target = jnp.sum(jnp.where(parent_front == parents[None, :], front_owner[None, :], 0), axis=1)
    rows_here = lax.dynamic_slice_in_dim(contrib_rows, place * share, share, 1) - place * height
    rows_here = jnp.where((target == column)[:, None], rows_here, -1).reshape(-1)
    selector = (
        lax.broadcasted_iota(jnp.int32, (height, rows_here.shape[0]), 0) == rows_here[None, :]
    ).astype(jnp.float32)
    positioned_rows = jnp.dot(
        selector,
        front_portions.reshape(-1, front_portions.shape[-1]),
        precision=EXACT,
        preferred_element_type=jnp.float32,
    )
    taken = jnp.max(selector, axis=1) > 0
    assembled = jnp.where(taken[:, None], positioned_rows, upper_rhs[0])[None]
    upper_applied = wy_apply(assembled, upper_vectors, upper_factors[:, 0])
    whole = jnp.full((1,), blocks, jnp.int32)
    upper_tops = run_tree(
        upper_applied[:, :width], summit_vectors[:, 0], summit_factors[:, 0], whole, place
    )
    upper_result = jnp.concatenate([upper_tops, upper_applied[:, width:]], axis=1)
    return (lower_result, upper_result)


def solution(mesh):
    placed = (
        P("fronts", "rows", None),
        P("fronts", "rows", None),
        P("fronts", "rows", None, None),
        P("fronts", "rows", None, None),
        P("fronts", "rows", None, None),
        P(),
        P(),
        P(),
        P(),
        P("fronts", "rows", None),
        P("fronts", "rows", None),
        P("fronts", "rows", None, None),
        P("fronts", "rows", None, None),
        P("fronts", "rows", None, None),
    )
    return jax.shard_map(
        per_device,
        mesh=mesh,
        in_specs=placed,
        out_specs=(P("fronts", "rows", None), P("fronts", "rows", None)),
        check_vma=False,
    )
```

profile of v0, /device:TPU:0, one launch (start us, length us, event | category | flops | bytes accessed | tf_op | source)
XLA Modules:
  0.0 505.6 jit_solution(8171327496330712370)
XLA Ops:
  7.2 5.5 %copy.94 = f32[2,1024,512]{1,2,0:T(8,128)} copy(f32[2,1024,512]{2,1,0:T(8,128)} %param.14) | data formatting | bytes 8388608 | tf_op args[0]
  12.7 8.5 %fusion.110 = f32[2,256,512]{1,2,0:T(8,128)S(1)} fusion(f32[2,1024,256]{2,1,0:T(8,128)S(1)} %copy-done, f32[2,1024,512]{2,1,0:T(8,128)} %param.14), kind=kOutput, calls=%fused_computation.174 | convolution fusion | flops 3221225472 | bytes 7340032 | tf_op jit(solution)/shard_map/fri,frn->fin/dot_general | solution.py:22
  21.3 2.1 fusion.32
  23.5 5.6 %subtract_select_fusion = f32[2,1024,512]{1,2,0:T(8,128)S(1)} fusion(f32[2,1024,512]{1,2,0:T(8,128)} %copy.94, f32[2,512,256]{2,1,0:T(8,128)S(1)} %fusion.32, f32[2,1024,256]{2,1,0:T(8,128)S(1)} %copy-done, pred[2]{0:T(512)(128)(4,1)S(1)} %get-tuple-element.11), kind=kOutput, calls=%fused_computation | convolution fusion | flops 3223322624 | bytes 11534338 | tf_op jit(solution)/shard_map/fri,fin->frn/dot_general | solution.py:24
  34.0 33.7 %collective-permute-done.2 = f32[2,256,256]{2,1,0:T(8,128)S(1)} collective-permute-done((f32[2,256,256]{2,1,0:T(8,128)S(1)}, f32[2,256,256]{2,1,0:T(8,128)S(1)}, u32[]{:S(2)}, u32[]{:S(2)}) %collective-permute-start.2) | collective-permute-done | bytes 524320 | tf_op jit(solution)/shard_map/ppermute | solution.py:13
  68.5 3.3 convolution_add_fusion.3
  71.8 5.9 %collective-permute-done.1 = f32[2,256,256]{2,1,0:T(8,128)} collective-permute-done((f32[2,256,256]{2,1,0:T(8,128)S(1)}, f32[2,256,256]{2,1,0:T(8,128)}, u32[]{:S(2)}, u32[]{:S(2)}) %collective-permute-start.1) | collective-permute-done | bytes 524320 | tf_op jit(solution)/shard_map/ppermute | solution.py:13
  77.8 3.0 fusion.40
  82.0 4.1 subtract_select_fusion.4
  86.1 3.4 collective-permute-start.3
  89.8 3.3 collective-permute-start.4
  93.0 32.0 %collective-permute-done.5 = f32[2,256,256]{2,1,0:T(8,128)S(1)} collective-permute-done((f32[2,256,256]{2,1,0:T(8,128)S(1)}, f32[2,256,256]{2,1,0:T(8,128)S(1)}, u32[]{:S(2)}, u32[]{:S(2)}) %collective-permute-start.5) | collective-permute-done | bytes 524320 | tf_op jit(solution)/shard_map/ppermute | solution.py:13
  126.4 7.9 %collective-permute-done.4 = f32[2,256,256]{2,1,0:T(8,128)S(1)} collective-permute-done((f32[2,256,256]{2,1,0:T(8,128)S(1)}, f32[2,256,256]{2,1,0:T(8,128)S(1)}, u32[]{:S(2)}, u32[]{:S(2)}) %collective-permute-start.4) | collective-permute-done | bytes 524320 | tf_op jit(solution)/shard_map/ppermute | solution.py:13
  134.3 1.9 fusion.38
  137.6 4.1 subtract_select_fusion.3
  141.7 2.2 collective-permute-start.6
  144.2 1.9 collective-permute-start.7
  146.1 33.0 %collective-permute-done.8 = f32[2,256,256]{2,1,0:T(8,128)S(1)} collective-permute-done((f32[2,256,256]{2,1,0:T(8,128)S(1)}, f32[2,256,256]{2,1,0:T(8,128)S(1)}, u32[]{:S(2)}, u32[]{:S(2)}) %collective-permute-start.8) | collective-permute-done | bytes 524320 | tf_op jit(solution)/shard_map/ppermute | solution.py:13
  180.5 7.3 %collective-permute-done.7 = f32[2,256,256]{2,1,0:T(8,128)S(1)} collective-permute-done((f32[2,256,256]{2,1,0:T(8,128)S(1)}, f32[2,256,256]{2,1,0:T(8,128)S(1)}, u32[]{:S(2)}, u32[]{:S(2)}) %collective-permute-start.7) | collective-permute-done | bytes 524320 | tf_op jit(solution)/shard_map/ppermute | solution.py:13
  187.8 1.9 fusion.36
  191.1 4.1 subtract_select_fusion.2
  195.2 3.8 collective-permute-start.9
  199.1 3.4 collective-permute-start.10
  202.5 31.8 %collective-permute-done.11 = f32[2,256,256]{2,1,0:T(8,128)} collective-permute-done((f32[2,256,256]{2,1,0:T(8,128)S(1)}, f32[2,256,256]{2,1,0:T(8,128)}, u32[]{:S(2)}, u32[]{:S(2)}) %collective-permute-start.11) | collective-permute-done | bytes 524320 | tf_op jit(solution)/shard_map/ppermute | solution.py:13
  234.3 2.7 convolution_add_fusion
  237.0 5.1 %collective-permute-done.10 = f32[2,256,256]{2,1,0:T(8,128)} collective-permute-done((f32[2,256,256]{2,1,0:T(8,128)S(1)}, f32[2,256,256]{2,1,0:T(8,128)}, u32[]{:S(2)}, u32[]{:S(2)}) %collective-permute-start.10) | collective-permute-done | bytes 524320 | tf_op jit(solution)/shard_map/ppermute | solution.py:13
  242.1 3.0 fusion.34
  246.5 5.0 broadcast_select_fusion
  252.8 87.2 %all-reduce.2.cloned.1.call-done = f32[2,128,512]{1,2,0:T(8,128)} async-done(((f32[2,128,512]{1,2,0:T(8,128)}), f32[2,128,512]{1,2,0:T(8,128)}) %all-reduce.2.cloned.1.call-update) | async-done | bytes 524304 | tf_op jit(solution)/shard_map/psum | solution.py:18
  340.0 2.0 copy.124
  342.5 31.2 %all-gather.2.cloned.1.call-done = f32[16,128,512]{2,1,0:T(8,128)} async-done(((f32[2,128,512]{2,1,0:T(8,128)}), f32[16,128,512]{2,1,0:T(8,128)}) %all-gather.2.cloned.1.call-update) | async-done | bytes 4194320 | tf_op jit(solution)/shard_map/all_gather | solution.py:82
  373.7 2.7 bitcast_select_fusion
  376.5 3.4 fusion.22
  380.5 1.9 fusion
  386.8 17.1 %collective-permute-done.14 = f32[1,256,256]{2,1,0:T(8,128)S(1)} collective-permute-done((f32[1,256,256]{2,1,0:T(8,128)S(1)}, f32[1,256,256]{2,1,0:T(8,128)S(1)}, u32[]{:S(2)}, u32[]{:S(2)}) %collective-permute-start.14) | collective-permute-done | bytes 262176 | tf_op jit(solution)/shard_map/ppermute | solution.py:13
  403.9 2.0 fusion.6
  405.9 2.9 collective-permute-done.13
  412.1 3.1 collective-permute-start.15
  415.8 3.1 collective-permute-start.16
  418.9 15.4 %collective-permute-done.17 = f32[1,256,256]{2,1,0:T(8,128)} collective-permute-done((f32[1,256,256]{2,1,0:T(8,128)S(1)}, f32[1,256,256]{2,1,0:T(8,128)}, u32[]{:S(2)}, u32[]{:S(2)}) %collective-permute-start.17) | collective-permute-done | bytes 262176 | tf_op jit(solution)/shard_map/ppermute | solution.py:13
  436.0 2.2 collective-permute-done.16
  445.5 16.8 %collective-permute-done.20 = f32[1,256,256]{2,1,0:T(8,128)S(1)} collective-permute-done((f32[1,256,256]{2,1,0:T(8,128)S(1)}, f32[1,256,256]{2,1,0:T(8,128)S(1)}, u32[]{:S(2)}, u32[]{:S(2)}) %collective-permute-start.20) | collective-permute-done | bytes 262176 | tf_op jit(solution)/shard_map/ppermute | solution.py:13
  463.0 2.0 fusion.14
  469.1 3.2 collective-permute-start.21
  472.7 3.2 collective-permute-start.22
  475.9 3.7 slice.21
  479.6 4.8 pad_maximum_fusion
  484.4 5.4 %copy.126 = f32[2,1024,512]{2,1,0:T(8,128)} copy(f32[2,1024,512]{1,2,0:T(8,128)} %pad_maximum_fusion) | data formatting | bytes 8388608
  (116 shorter events, 48.0 us)
Async XLA Ops:
  7.2 5.6 %copy-start = (f32[2,1024,256]{2,1,0:T(8,128)S(1)}, f32[2,1024,256]{2,1,0:T(8,128)}, u32[]{:S(2)}) copy-start(f32[2,1024,256]{2,1,0:T(8,128)} %param.15) | copy-start | bytes 6291460
  7.2 332.8 %all-reduce.2.cloned.1.call-start = ((), (), s32[]{:S(2)}) async-start(), calls=%async_computation | async-start | bytes 1048576 | tf_op jit(solution)/shard_map/psum | solution.py:18
  21.3 2.2 copy-start.24
  29.1 2.7 copy-start.3
  29.1 2.7 copy-start.2
  29.1 3.9 copy-start.9
  30.2 37.5 %collective-permute-start = (f32[2,256,512]{1,2,0:T(8,128)}, f32[2,256,512]{1,2,0:T(8,128)S(1)}, u32[]{:S(2)}, u32[]{:S(2)}) collective-permute-start(f32[2,256,512]{1,2,0:T(8,128)} %slice.20), channel_id=1, source_target_pairs={{0,1},{1,0},{2,3},{3,2},{4,5},{5,4},{6,7},{7,6},{8,9},{9,8},{10,11... | collective-permute-start | bytes 3145736 | tf_op jit(solution)/shard_map/ppermute | solution.py:13
  31.8 35.9 %collective-permute-start.2 = (f32[2,256,256]{2,1,0:T(8,128)S(1)}, f32[2,256,256]{2,1,0:T(8,128)S(1)}, u32[]{:S(2)}, u32[]{:S(2)}) collective-permute-start(f32[2,256,256]{2,1,0:T(8,128)S(1)} %bitcast.283), channel_id=1, source_target_pairs={{0,1},{1,0},{2,3},{3,2},{4,5},{5,4},{6,7},{7,6},{8,9},{9,8},{10,11... | collective-permute-start | bytes 1572872 | tf_op jit(solution)/shard_map/ppermute | solution.py:13
  33.0 44.7 %collective-permute-start.1 = (f32[2,256,256]{2,1,0:T(8,128)S(1)}, f32[2,256,256]{2,1,0:T(8,128)}, u32[]{:S(2)}, u32[]{:S(2)}) collective-permute-start(f32[2,256,256]{2,1,0:T(8,128)S(1)} %bitcast.291), channel_id=1, source_target_pairs={{0,1},{1,0},{2,3},{3,2},{4,5},{5,4},{6,7},{7,6},{8,9},{9,8},{10,11... | collective-permute-start | bytes 1572872 | tf_op jit(solution)/shard_map/ppermute | solution.py:13
  68.5 3.3 copy-start.11
  86.1 38.9 %collective-permute-start.3 = (f32[2,256,512]{1,2,0:T(8,128)S(1)}, f32[2,256,512]{1,2,0:T(8,128)S(1)}, u32[]{:S(2)}, u32[]{:S(2)}) collective-permute-start(f32[2,256,512]{1,2,0:T(8,128)S(1)} %subtract_select_fusion.4), channel_id=1, source_target_pairs={{0,2},{1,3},{2,0},{3,1},{4,6},{5,7},{6,4},{7,5},{8,10},{9,11},{10,... | collective-permute-start | bytes 3145736 | tf_op jit(solution)/shard_map/ppermute | solution.py:13
  89.5 35.5 %collective-permute-start.5 = (f32[2,256,256]{2,1,0:T(8,128)S(1)}, f32[2,256,256]{2,1,0:T(8,128)S(1)}, u32[]{:S(2)}, u32[]{:S(2)}) collective-permute-start(f32[2,256,256]{2,1,0:T(8,128)S(1)} %bitcast.284), channel_id=1, source_target_pairs={{0,2},{1,3},{2,0},{3,1},{4,6},{5,7},{6,4},{7,5},{8,10},{9,11},{10,... | collective-permute-start | bytes 1572872 | tf_op jit(solution)/shard_map/ppermute | solution.py:13
  89.8 44.5 %collective-permute-start.4 = (f32[2,256,256]{2,1,0:T(8,128)S(1)}, f32[2,256,256]{2,1,0:T(8,128)S(1)}, u32[]{:S(2)}, u32[]{:S(2)}) collective-permute-start(f32[2,256,256]{2,1,0:T(8,128)S(1)} %bitcast.292), channel_id=1, source_target_pairs={{0,2},{1,3},{2,0},{3,1},{4,6},{5,7},{6,4},{7,5},{8,10},{9,11},{10,... | collective-permute-start | bytes 1572872 | tf_op jit(solution)/shard_map/ppermute | solution.py:13
  125.0 1.4 copy-start.18
  125.0 1.4 copy-start.14
  141.7 37.5 %collective-permute-start.6 = (f32[2,256,512]{1,2,0:T(8,128)S(1)}, f32[2,256,512]{1,2,0:T(8,128)S(1)}, u32[]{:S(2)}, u32[]{:S(2)}) collective-permute-start(f32[2,256,512]{1,2,0:T(8,128)S(1)} %subtract_select_fusion.3), channel_id=1, source_target_pairs={{0,4},{1,5},{2,6},{3,7},{4,0},{5,1},{6,2},{7,3},{8,12},{9,13},{10,... | collective-permute-start | bytes 3145736 | tf_op jit(solution)/shard_map/ppermute | solution.py:13
  143.9 35.2 %collective-permute-start.8 = (f32[2,256,256]{2,1,0:T(8,128)S(1)}, f32[2,256,256]{2,1,0:T(8,128)S(1)}, u32[]{:S(2)}, u32[]{:S(2)}) collective-permute-start(f32[2,256,256]{2,1,0:T(8,128)S(1)} %bitcast.285), channel_id=1, source_target_pairs={{0,4},{1,5},{2,6},{3,7},{4,0},{5,1},{6,2},{7,3},{8,12},{9,13},{10,... | collective-permute-start | bytes 1572872 | tf_op jit(solution)/shard_map/ppermute | solution.py:13
  144.2 43.6 %collective-permute-start.7 = (f32[2,256,256]{2,1,0:T(8,128)S(1)}, f32[2,256,256]{2,1,0:T(8,128)S(1)}, u32[]{:S(2)}, u32[]{:S(2)}) collective-permute-start(f32[2,256,256]{2,1,0:T(8,128)S(1)} %bitcast.293), channel_id=1, source_target_pairs={{0,4},{1,5},{2,6},{3,7},{4,0},{5,1},{6,2},{7,3},{8,12},{9,13},{10,... | collective-permute-start | bytes 1572872 | tf_op jit(solution)/shard_map/ppermute | solution.py:13
  195.2 39.1 %collective-permute-start.9 = (f32[2,256,512]{1,2,0:T(8,128)S(1)}, f32[2,256,512]{1,2,0:T(8,128)S(1)}, u32[]{:S(2)}, u32[]{:S(2)}) collective-permute-start(f32[2,256,512]{1,2,0:T(8,128)S(1)} %subtract_select_fusion.2), channel_id=1, source_target_pairs={{0,8},{1,9},{2,10},{3,11},{4,12},{5,13},{6,14},{7,15},{8,0},{9,1},... | collective-permute-start | bytes 3145736 | tf_op jit(solution)/shard_map/ppermute | solution.py:13
  199.0 35.4 %collective-permute-start.11 = (f32[2,256,256]{2,1,0:T(8,128)S(1)}, f32[2,256,256]{2,1,0:T(8,128)}, u32[]{:S(2)}, u32[]{:S(2)}) collective-permute-start(f32[2,256,256]{2,1,0:T(8,128)S(1)} %bitcast.286), channel_id=1, source_target_pairs={{0,8},{1,9},{2,10},{3,11},{4,12},{5,13},{6,14},{7,15},{8,0},{9,1},... | collective-permute-start | bytes 1572872 | tf_op jit(solution)/shard_map/ppermute | solution.py:13
  199.1 43.1 %collective-permute-start.10 = (f32[2,256,256]{2,1,0:T(8,128)S(1)}, f32[2,256,256]{2,1,0:T(8,128)}, u32[]{:S(2)}, u32[]{:S(2)}) collective-permute-start(f32[2,256,256]{2,1,0:T(8,128)S(1)} %bitcast.294), channel_id=1, source_target_pairs={{0,8},{1,9},{2,10},{3,11},{4,12},{5,13},{6,14},{7,15},{8,0},{9,1},... | collective-permute-start | bytes 1572872 | tf_op jit(solution)/shard_map/ppermute | solution.py:13
  234.3 2.7 copy-start.12
  251.5 90.6 %copy-start.25 = (s32[8]{0:T(128)S(1)}, s32[8]{0:T(128)}, u32[]{:S(2)}) copy-start(s32[8]{0:T(128)} %param.21) | copy-start | bytes 100
  251.5 90.6 %copy-start.26 = (s32[16,1]{0,1:T(1,128)S(1)}, s32[16,1]{0,1:T(1,128)}, u32[]{:S(2)}) copy-start(s32[16,1]{0,1:T(1,128)} %param.20) | copy-start | bytes 196
  251.5 90.7 %copy-start.23 = (s32[16,128]{1,0:T(8,128)S(1)}, s32[16,128]{1,0:T(8,128)}, u32[]{:S(2)}) copy-start(s32[16,128]{1,0:T(8,128)} %param.22) | copy-start | bytes 24580
  252.3 121.4 %all-gather.2.cloned.1.call-start = ((), (), s32[]{:S(2)}) async-start(), calls=%async_computation.1 | async-start | bytes 4718592 | tf_op jit(solution)/shard_map/all_gather | solution.py:82
  342.5 33.9 %copy-start.10 = (f32[1,1024,256]{2,1,0:T(8,128)S(1)}, f32[1,1024,256]{2,1,0:T(8,128)}, u32[]{:S(2)}) copy-start(f32[1,1024,256]{2,1,0:T(8,128)} %param.24) | copy-start | bytes 3145732
  376.4 3.5 copy-start.22
  380.5 4.3 copy-start.4
  382.4 2.4 copy-start.5
  383.3 20.6 %collective-permute-start.12 = (f32[1,256,512]{2,1,0:T(8,128)}, f32[1,256,512]{2,1,0:T(8,128)S(1)}, u32[]{:S(2)}, u32[]{:S(2)}) collective-permute-start(f32[1,256,512]{2,1,0:T(8,128)} %slice.23), channel_id=1, source_target_pairs={{0,1},{1,0},{2,3},{3,2},{4,5},{5,4},{6,7},{7,6},{8,9},{9,8},{10,11... | collective-permute-start | bytes 1572872 | tf_op jit(solution)/shard_map/ppermute | solution.py:13
  384.8 25.6 %copy-start.6 = (f32[1,1024,512]{2,1,0:T(8,128)S(1)}, f32[1,1024,512]{2,1,0:T(8,128)}, u32[]{:S(2)}) copy-start(f32[1,1024,512]{2,1,0:T(8,128)} %copy-done.5) | copy-start | bytes 6291460
  384.8 19.1 %collective-permute-start.14 = (f32[1,256,256]{2,1,0:T(8,128)S(1)}, f32[1,256,256]{2,1,0:T(8,128)S(1)}, u32[]{:S(2)}, u32[]{:S(2)}) collective-permute-start(f32[1,256,256]{2,1,0:T(8,128)S(1)} %bitcast.287), channel_id=1, source_target_pairs={{0,1},{1,0},{2,3},{3,2},{4,5},{5,4},{6,7},{7,6},{8,9},{9,8},{10,11... | collective-permute-start | bytes 786440 | tf_op jit(solution)/shard_map/ppermute | solution.py:13
  385.4 23.4 %collective-permute-start.13 = (f32[1,256,256]{2,1,0:T(8,128)}, f32[1,256,256]{2,1,0:T(8,128)S(1)}, u32[]{:S(2)}, u32[]{:S(2)}) collective-permute-start(f32[1,256,256]{2,1,0:T(8,128)} %bitcast.11), channel_id=1, source_target_pairs={{0,1},{1,0},{2,3},{3,2},{4,5},{5,4},{6,7},{7,6},{8,9},{9,8},{10,11... | collective-permute-start | bytes 786440 | tf_op jit(solution)/shard_map/ppermute | solution.py:13
  403.9 4.9 copy-start.19
  412.1 22.1 %collective-permute-start.15 = (f32[1,256,512]{2,1,0:T(8,128)S(1)}, f32[1,256,512]{2,1,0:T(8,128)S(1)}, u32[]{:S(2)}, u32[]{:S(2)}) collective-permute-start(f32[1,256,512]{2,1,0:T(8,128)S(1)} %fusion.30), channel_id=1, source_target_pairs={{0,2},{1,3},{2,0},{3,1},{4,6},{5,7},{6,4},{7,5},{8,10},{9,11},{10,... | collective-permute-start | bytes 1572872 | tf_op jit(solution)/shard_map/ppermute | solution.py:13
  415.2 19.0 %collective-permute-start.17 = (f32[1,256,256]{2,1,0:T(8,128)S(1)}, f32[1,256,256]{2,1,0:T(8,128)}, u32[]{:S(2)}, u32[]{:S(2)}) collective-permute-start(f32[1,256,256]{2,1,0:T(8,128)S(1)} %bitcast.288), channel_id=1, source_target_pairs={{0,2},{1,3},{2,0},{3,1},{4,6},{5,7},{6,4},{7,5},{8,10},{9,11},{10,... | collective-permute-start | bytes 786440 | tf_op jit(solution)/shard_map/ppermute | solution.py:13
  415.8 22.5 %collective-permute-start.16 = (f32[1,256,256]{2,1,0:T(8,128)}, f32[1,256,256]{2,1,0:T(8,128)}, u32[]{:S(2)}, u32[]{:S(2)}) collective-permute-start(f32[1,256,256]{2,1,0:T(8,128)} %bitcast.11), channel_id=1, source_target_pairs={{0,2},{1,3},{2,0},{3,1},{4,6},{5,7},{6,4},{7,5},{8,10},{9,11},{10,... | collective-permute-start | bytes 786440 | tf_op jit(solution)/shard_map/ppermute | solution.py:13
  434.2 4.0 copy-start.16
  441.8 21.2 %collective-permute-start.18 = (f32[1,256,512]{2,1,0:T(8,128)S(1)}, f32[1,256,512]{2,1,0:T(8,128)}, u32[]{:S(2)}, u32[]{:S(2)}) collective-permute-start(f32[1,256,512]{2,1,0:T(8,128)S(1)} %fusion.28), channel_id=1, source_target_pairs={{0,4},{1,5},{2,6},{3,7},{4,0},{5,1},{6,2},{7,3},{8,12},{9,13},{10,... | collective-permute-start | bytes 1572872 | tf_op jit(solution)/shard_map/ppermute | solution.py:13
  443.5 18.9 %collective-permute-start.20 = (f32[1,256,256]{2,1,0:T(8,128)S(1)}, f32[1,256,256]{2,1,0:T(8,128)S(1)}, u32[]{:S(2)}, u32[]{:S(2)}) collective-permute-start(f32[1,256,256]{2,1,0:T(8,128)S(1)} %bitcast.289), channel_id=1, source_target_pairs={{0,4},{1,5},{2,6},{3,7},{4,0},{5,1},{6,2},{7,3},{8,12},{9,13},{10,... | collective-permute-start | bytes 786440 | tf_op jit(solution)/shard_map/ppermute | solution.py:13
  444.0 21.7 %collective-permute-start.19 = (f32[1,256,256]{2,1,0:T(8,128)}, f32[1,256,256]{2,1,0:T(8,128)}, u32[]{:S(2)}, u32[]{:S(2)}) collective-permute-start(f32[1,256,256]{2,1,0:T(8,128)} %bitcast.11), channel_id=1, source_target_pairs={{0,4},{1,5},{2,6},{3,7},{4,0},{5,1},{6,2},{7,3},{8,12},{9,13},{10,... | collective-permute-start | bytes 786440 | tf_op jit(solution)/shard_map/ppermute | solution.py:13
  463.0 4.3 copy-start.21
  469.1 21.6 %collective-permute-start.21 = (f32[1,256,512]{2,1,0:T(8,128)S(1)}, f32[1,256,512]{2,1,0:T(8,128)S(1)}, u32[]{:S(2)}, u32[]{:S(2)}) collective-permute-start(f32[1,256,512]{2,1,0:T(8,128)S(1)} %fusion.26), channel_id=1, source_target_pairs={{0,8},{1,9},{2,10},{3,11},{4,12},{5,13},{6,14},{7,15},{8,0},{9,1},... | collective-permute-start | bytes 1572872 | tf_op jit(solution)/shard_map/ppermute | solution.py:13
  472.3 18.4 %collective-permute-start.23 = (f32[1,256,256]{2,1,0:T(8,128)S(1)}, f32[1,256,256]{2,1,0:T(8,128)}, u32[]{:S(2)}, u32[]{:S(2)}) collective-permute-start(f32[1,256,256]{2,1,0:T(8,128)S(1)} %bitcast.290), channel_id=1, source_target_pairs={{0,8},{1,9},{2,10},{3,11},{4,12},{5,13},{6,14},{7,15},{8,0},{9,1},... | collective-permute-start | bytes 786440 | tf_op jit(solution)/shard_map/ppermute | solution.py:13
  472.7 20.8 %collective-permute-start.22 = (f32[1,256,256]{2,1,0:T(8,128)}, f32[1,256,256]{2,1,0:T(8,128)}, u32[]{:S(2)}, u32[]{:S(2)}) collective-permute-start(f32[1,256,256]{2,1,0:T(8,128)} %bitcast.11), channel_id=1, source_target_pairs={{0,8},{1,9},{2,10},{3,11},{4,12},{5,13},{6,14},{7,15},{8,0},{9,1},... | collective-permute-start | bytes 786440 | tf_op jit(solution)/shard_map/ppermute | solution.py:13
  492.3 4.7 slice-start
  495.2 3.4 copy-start.1
  (6 other events, 6.8 us)
Sparse Core Ops, SparseCore 0:
  252.5 87.4 all-reduce.1
  342.3 31.4 all-gather.1
where the time goes:
time: 512 us; the launch traced here: 506 us
  waiting for transfers between devices  332 us (65%)
  matrix products  81.7 us (16%)
  starting transfers between devices  43.5 us (8%)
  local copies, waits for them, and re-layouts  25.6 us (5%)
  between operations  14.8 us (3%)
  other arithmetic  7.53 us (1%)
    ppermute x24, waiting for transfers between devices, partner(): return lax.ppermute(value, axis, pairs)  214 us
    psum x1, waiting for transfers between devices, from_root(): return lax.psum(kept, axis)  87.2 us
    ppermute x24, starting transfers between devices, partner(): return lax.ppermute(value, axis, pairs)  43 us
    all_gather x1, waiting for transfers between devices, per_device(): gathered = lax.all_gather(shared, 'fronts', axis=0, tiled=True)  31.2 us
    dot_general x8, matrix products, combine(): jnp.einsum('fij,fjn->fin', vectors, weight, precision=EXACT)  24.5 us
    dot_general x8, matrix products, combine(): weight = jnp.einsum('fij,fin->fjn', factors, inner, precision=EXACT)  16.4 us
    dot_general x8, matrix products, combine(): inner = lead + jnp.einsum('fij,fin->fjn', vectors, rest, precision=EXACT)  16 us
    unnamed x56, local copies, waits for them, and re-layouts  12.5 us
  transfers between devices with their start and end apart: 26, of which 18 were waited for; matrix products, arithmetic and copies ran while one was open for 6% of the time, Pallas kernels for 0%

commit v1 on v0

--- a/solution.py
+++ b/solution.py
@@ -79,7 +79,9 @@
     contrib = tops[:, NPIV:]
     share = (width - NPIV) // blocks
     shared = from_root(contrib, "rows", 0)
-    gathered = lax.all_gather(shared, "fronts", axis=0, tiled=True)
+    gathered = jnp.concatenate(
+        lax.all_to_all(jnp.stack([shared] * lax.axis_size("fronts")), "fronts", 0, 0), axis=0
+    )
     front_portions = lax.dynamic_slice_in_dim(gathered, place * share, share, 1)
     parents = jnp.arange(front_owner.shape[0], dtype=jnp.int32)
     target = jnp.sum(jnp.where(parent_front == parents[None, :], front_owner[None, :], 0), axis=1)

time: 512 us -> 533 us (1.041)
  waiting for transfers between devices: 332 us -> 352 us
    all_to_all x0 -> x1, waiting for transfers between devices: none -> 49.2 us  [per_device(): lax.all_to_all(jnp.stack([shared] * lax.axis_size('fronts')), 'fronts', 0...]
    all_gather x1 -> x0, waiting for transfers between devices: 31.2 us -> none  [per_device(): gathered = lax.all_gather(shared, 'fronts', axis=0, tiled=True)]
    unnamed x56 -> x60, local copies, waits for them, and re-layouts: 12.5 us -> 12.5 us
  transfers between devices with their start and end apart: 26 -> 26, of which waited for: 18 -> 18; matrix products, arithmetic and copies ran while one was open for 6% -> 5% of each run, Pallas kernels for 0% -> 0%
where the time goes in v1:
time: 533 us; the launch traced here: 527 us
  waiting for transfers between devices  352 us (66%)
  matrix products  80.9 us (15%)
  starting transfers between devices  45.9 us (9%)
  local copies, waits for them, and re-layouts  25.5 us (5%)
  between operations  14.8 us (3%)
  other arithmetic  7.52 us (1%)
    ppermute x24, waiting for transfers between devices, partner(): return lax.ppermute(value, axis, pairs)  215 us
    psum x1, waiting for transfers between devices, from_root(): return lax.psum(kept, axis)  87.7 us
    all_to_all x1, waiting for transfers between devices, per_device(): lax.all_to_all(jnp.stack([shared] * lax.axis_size('fronts')), 'fronts', 0...  49.2 us
    ppermute x24, starting transfers between devices, partner(): return lax.ppermute(value, axis, pairs)  40.7 us
    dot_general x8, matrix products, combine(): jnp.einsum('fij,fjn->fin', vectors, weight, precision=EXACT)  24.4 us
    dot_general x8, matrix products, combine(): weight = jnp.einsum('fij,fin->fjn', factors, inner, precision=EXACT)  16.6 us
    dot_general x8, matrix products, combine(): inner = lead + jnp.einsum('fij,fin->fjn', vectors, rest, precision=EXACT)  16 us
    unnamed x60, local copies, waits for them, and re-layouts  12.5 us
  transfers between devices with their start and end apart: 26, of which 18 were waited for; matrix products, arithmetic and copies ran while one was open for 5% of the time, Pallas kernels for 0%

profile of v1, /device:TPU:0, one launch (start us, length us, event | category | flops | bytes accessed | tf_op | source)
XLA Modules:
  0.0 526.6 jit_solution(2491099389419857637)
XLA Ops:
  7.2 5.5 %copy.60 = f32[2,1024,512]{1,2,0:T(8,128)} copy(f32[2,1024,512]{2,1,0:T(8,128)} %param.14) | data formatting | bytes 8388608 | tf_op args[0]
  12.7 8.6 %fusion.110 = f32[2,256,512]{1,2,0:T(8,128)S(1)} fusion(f32[2,1024,256]{2,1,0:T(8,128)S(1)} %copy-done, f32[2,1024,512]{2,1,0:T(8,128)} %param.14), kind=kOutput, calls=%fused_computation.174 | convolution fusion | flops 3221225472 | bytes 7340032 | tf_op jit(solution)/shard_map/fri,frn->fin/dot_general | solution.py:22
  22.5 5.6 %subtract_select_fusion = f32[2,1024,512]{1,2,0:T(8,128)S(1)} fusion(f32[2,1024,512]{1,2,0:T(8,128)} %copy.60, f32[2,512,256]{2,1,0:T(8,128)S(1)} %fusion.32, f32[2,1024,256]{2,1,0:T(8,128)S(1)} %copy-done, pred[2]{0:T(512)(128)(4,1)S(1)} %get-tuple-element.9), kind=kOutput, calls=%fused_computation | convolution fusion | flops 3223322624 | bytes 11534338 | tf_op jit(solution)/shard_map/fri,fin->frn/dot_general | solution.py:24
  33.1 33.7 %collective-permute-done.2 = f32[2,256,256]{2,1,0:T(8,128)S(1)} collective-permute-done((f32[2,256,256]{2,1,0:T(8,128)S(1)}, f32[2,256,256]{2,1,0:T(8,128)S(1)}, u32[]{:S(2)}, u32[]{:S(2)}) %collective-permute-start.2) | collective-permute-done | bytes 524320 | tf_op jit(solution)/shard_map/ppermute | solution.py:13
  67.5 3.3 convolution_add_fusion.3
  70.9 5.9 %collective-permute-done.1 = f32[2,256,256]{2,1,0:T(8,128)} collective-permute-done((f32[2,256,256]{2,1,0:T(8,128)S(1)}, f32[2,256,256]{2,1,0:T(8,128)}, u32[]{:S(2)}, u32[]{:S(2)}) %collective-permute-start.1) | collective-permute-done | bytes 524320 | tf_op jit(solution)/shard_map/ppermute | solution.py:13
  76.8 3.0 fusion.40
  81.1 4.1 subtract_select_fusion.4
  85.2 3.4 collective-permute-start.3
  88.8 3.3 collective-permute-start.4
  92.1 32.0 %collective-permute-done.5 = f32[2,256,256]{2,1,0:T(8,128)S(1)} collective-permute-done((f32[2,256,256]{2,1,0:T(8,128)S(1)}, f32[2,256,256]{2,1,0:T(8,128)S(1)}, u32[]{:S(2)}, u32[]{:S(2)}) %collective-permute-start.5) | collective-permute-done | bytes 524320 | tf_op jit(solution)/shard_map/ppermute | solution.py:13
  125.4 7.9 %collective-permute-done.4 = f32[2,256,256]{2,1,0:T(8,128)S(1)} collective-permute-done((f32[2,256,256]{2,1,0:T(8,128)S(1)}, f32[2,256,256]{2,1,0:T(8,128)S(1)}, u32[]{:S(2)}, u32[]{:S(2)}) %collective-permute-start.4) | collective-permute-done | bytes 524320 | tf_op jit(solution)/shard_map/ppermute | solution.py:13
  133.3 1.9 fusion.38
  136.6 4.1 subtract_select_fusion.3
  140.7 2.2 collective-permute-start.6
  143.2 1.9 collective-permute-start.7
  145.1 33.0 %collective-permute-done.8 = f32[2,256,256]{2,1,0:T(8,128)S(1)} collective-permute-done((f32[2,256,256]{2,1,0:T(8,128)S(1)}, f32[2,256,256]{2,1,0:T(8,128)S(1)}, u32[]{:S(2)}, u32[]{:S(2)}) %collective-permute-start.8) | collective-permute-done | bytes 524320 | tf_op jit(solution)/shard_map/ppermute | solution.py:13
  179.5 7.3 %collective-permute-done.7 = f32[2,256,256]{2,1,0:T(8,128)S(1)} collective-permute-done((f32[2,256,256]{2,1,0:T(8,128)S(1)}, f32[2,256,256]{2,1,0:T(8,128)S(1)}, u32[]{:S(2)}, u32[]{:S(2)}) %collective-permute-start.7) | collective-permute-done | bytes 524320 | tf_op jit(solution)/shard_map/ppermute | solution.py:13
  186.8 1.9 fusion.36
  190.1 4.1 subtract_select_fusion.2
  194.2 3.8 collective-permute-start.9
  198.1 3.7 collective-permute-start.10
  201.8 31.6 %collective-permute-done.11 = f32[2,256,256]{2,1,0:T(8,128)} collective-permute-done((f32[2,256,256]{2,1,0:T(8,128)S(1)}, f32[2,256,256]{2,1,0:T(8,128)}, u32[]{:S(2)}, u32[]{:S(2)}) %collective-permute-start.11) | collective-permute-done | bytes 524320 | tf_op jit(solution)/shard_map/ppermute | solution.py:13
  233.4 2.7 convolution_add_fusion
  236.1 5.1 collective-permute-done.10
  241.2 3.0 fusion.34
  245.4 4.9 broadcast_select_fusion
  251.2 87.7 %all-reduce.2.cloned.1.call-done = f32[2,128,512]{1,2,0:T(8,128)} async-done(((f32[2,128,512]{1,2,0:T(8,128)}), f32[2,128,512]{1,2,0:T(8,128)}) %all-reduce.2.cloned.1.call-update) | async-done | bytes 524304 | tf_op jit(solution)/shard_map/psum | solution.py:18
  340.2 2.5 stack.2
  342.7 5.1 all-to-all-start
  348.3 49.2 %all-to-all-done = f32[8,2,128,512]{3,2,1,0:T(8,128)} async-done(((f32[8,2,128,512]{3,2,1,0:T(8,128)}), f32[8,2,128,512]{3,2,1,0:T(8,128)}, u32[]{:S(2)}, u32[]{:S(2)}) %all-to-all-start) | async-done | bytes 4194336 | tf_op jit(solution)/shard_map/all_to_all | solution.py:83
  397.5 2.8 bitcast_select_fusion
  400.3 3.5 fusion.22
  404.4 1.9 fusion
  410.4 17.4 %collective-permute-done.14 = f32[1,256,256]{2,1,0:T(8,128)S(1)} collective-permute-done((f32[1,256,256]{2,1,0:T(8,128)S(1)}, f32[1,256,256]{2,1,0:T(8,128)S(1)}, u32[]{:S(2)}, u32[]{:S(2)}) %collective-permute-start.14) | collective-permute-done | bytes 262176 | tf_op jit(solution)/shard_map/ppermute | solution.py:13
  427.8 2.0 fusion.6
  429.8 2.2 collective-permute-done.13
  435.3 2.2 collective-permute-start.15
  439.0 2.3 collective-permute-start.16
  441.2 16.2 %collective-permute-done.17 = f32[1,256,256]{2,1,0:T(8,128)} collective-permute-done((f32[1,256,256]{2,1,0:T(8,128)S(1)}, f32[1,256,256]{2,1,0:T(8,128)}, u32[]{:S(2)}, u32[]{:S(2)}) %collective-permute-start.17) | collective-permute-done | bytes 262176 | tf_op jit(solution)/shard_map/ppermute | solution.py:13
  467.6 16.9 %collective-permute-done.20 = f32[1,256,256]{2,1,0:T(8,128)S(1)} collective-permute-done((f32[1,256,256]{2,1,0:T(8,128)S(1)}, f32[1,256,256]{2,1,0:T(8,128)S(1)}, u32[]{:S(2)}, u32[]{:S(2)}) %collective-permute-start.20) | collective-permute-done | bytes 262176 | tf_op jit(solution)/shard_map/ppermute | solution.py:13
  485.2 2.0 fusion.14
  491.1 2.2 collective-permute-start.21
  494.7 2.1 collective-permute-start.22
  496.8 2.0 slice.21
  498.7 4.8 pad_maximum_fusion
  503.5 5.4 %copy.92 = f32[2,1024,512]{2,1,0:T(8,128)} copy(f32[2,1024,512]{1,2,0:T(8,128)} %pad_maximum_fusion) | data formatting | bytes 8388608
  508.9 2.9 collective-permute-done.23
  (120 shorter events, 51.4 us)
Async XLA Ops:
  7.2 5.6 %copy-start = (f32[2,1024,256]{2,1,0:T(8,128)S(1)}, f32[2,1024,256]{2,1,0:T(8,128)}, u32[]{:S(2)}) copy-start(f32[2,1024,256]{2,1,0:T(8,128)} %param.15) | copy-start | bytes 6291460
  7.2 331.7 %all-reduce.2.cloned.1.call-start = ((), (), s32[]{:S(2)}) async-start(), calls=%async_computation.1 | async-start | bytes 1048576 | tf_op jit(solution)/shard_map/psum | solution.py:18
  12.7 8.6 %copy-start.23 = (f32[2,1,256,256]{3,2,1,0:T(8,128)S(1)}, f32[2,1,256,256]{3,2,1,0:T(8,128)}, u32[]{:S(2)}) copy-start(f32[2,1,256,256]{3,2,1,0:T(8,128)} %param.16) | copy-start | bytes 1572868
  28.1 2.7 copy-start.3
  28.1 2.7 copy-start.2
  28.1 3.9 copy-start.10
  29.2 37.5 %collective-permute-start = (f32[2,256,512]{1,2,0:T(8,128)}, f32[2,256,512]{1,2,0:T(8,128)S(1)}, u32[]{:S(2)}, u32[]{:S(2)}) collective-permute-start(f32[2,256,512]{1,2,0:T(8,128)} %slice.20), channel_id=1, source_target_pairs={{0,1},{1,0},{2,3},{3,2},{4,5},{5,4},{6,7},{7,6},{8,9},{9,8},{10,11... | collective-permute-start | bytes 3145736 | tf_op jit(solution)/shard_map/ppermute | solution.py:13
  30.8 35.9 %collective-permute-start.2 = (f32[2,256,256]{2,1,0:T(8,128)S(1)}, f32[2,256,256]{2,1,0:T(8,128)S(1)}, u32[]{:S(2)}, u32[]{:S(2)}) collective-permute-start(f32[2,256,256]{2,1,0:T(8,128)S(1)} %bitcast.284), channel_id=1, source_target_pairs={{0,1},{1,0},{2,3},{3,2},{4,5},{5,4},{6,7},{7,6},{8,9},{9,8},{10,11... | collective-permute-start | bytes 1572872 | tf_op jit(solution)/shard_map/ppermute | solution.py:13
  32.1 44.7 %collective-permute-start.1 = (f32[2,256,256]{2,1,0:T(8,128)S(1)}, f32[2,256,256]{2,1,0:T(8,128)}, u32[]{:S(2)}, u32[]{:S(2)}) collective-permute-start(f32[2,256,256]{2,1,0:T(8,128)S(1)} %bitcast.292), channel_id=1, source_target_pairs={{0,1},{1,0},{2,3},{3,2},{4,5},{5,4},{6,7},{7,6},{8,9},{9,8},{10,11... | collective-permute-start | bytes 1572872 | tf_op jit(solution)/shard_map/ppermute | solution.py:13
  67.5 3.3 copy-start.12
  85.2 38.9 %collective-permute-start.3 = (f32[2,256,512]{1,2,0:T(8,128)S(1)}, f32[2,256,512]{1,2,0:T(8,128)S(1)}, u32[]{:S(2)}, u32[]{:S(2)}) collective-permute-start(f32[2,256,512]{1,2,0:T(8,128)S(1)} %subtract_select_fusion.4), channel_id=1, source_target_pairs={{0,2},{1,3},{2,0},{3,1},{4,6},{5,7},{6,4},{7,5},{8,10},{9,11},{10,... | collective-permute-start | bytes 3145736 | tf_op jit(solution)/shard_map/ppermute | solution.py:13
  88.5 35.5 %collective-permute-start.5 = (f32[2,256,256]{2,1,0:T(8,128)S(1)}, f32[2,256,256]{2,1,0:T(8,128)S(1)}, u32[]{:S(2)}, u32[]{:S(2)}) collective-permute-start(f32[2,256,256]{2,1,0:T(8,128)S(1)} %bitcast.285), channel_id=1, source_target_pairs={{0,2},{1,3},{2,0},{3,1},{4,6},{5,7},{6,4},{7,5},{8,10},{9,11},{10,... | collective-permute-start | bytes 1572872 | tf_op jit(solution)/shard_map/ppermute | solution.py:13
  88.8 44.5 %collective-permute-start.4 = (f32[2,256,256]{2,1,0:T(8,128)S(1)}, f32[2,256,256]{2,1,0:T(8,128)S(1)}, u32[]{:S(2)}, u32[]{:S(2)}) collective-permute-start(f32[2,256,256]{2,1,0:T(8,128)S(1)} %bitcast.293), channel_id=1, source_target_pairs={{0,2},{1,3},{2,0},{3,1},{4,6},{5,7},{6,4},{7,5},{8,10},{9,11},{10,... | collective-permute-start | bytes 1572872 | tf_op jit(solution)/shard_map/ppermute | solution.py:13
  124.0 1.4 copy-start.15
  140.7 37.5 %collective-permute-start.6 = (f32[2,256,512]{1,2,0:T(8,128)S(1)}, f32[2,256,512]{1,2,0:T(8,128)S(1)}, u32[]{:S(2)}, u32[]{:S(2)}) collective-permute-start(f32[2,256,512]{1,2,0:T(8,128)S(1)} %subtract_select_fusion.3), channel_id=1, source_target_pairs={{0,4},{1,5},{2,6},{3,7},{4,0},{5,1},{6,2},{7,3},{8,12},{9,13},{10,... | collective-permute-start | bytes 3145736 | tf_op jit(solution)/shard_map/ppermute | solution.py:13
  142.9 35.2 %collective-permute-start.8 = (f32[2,256,256]{2,1,0:T(8,128)S(1)}, f32[2,256,256]{2,1,0:T(8,128)S(1)}, u32[]{:S(2)}, u32[]{:S(2)}) collective-permute-start(f32[2,256,256]{2,1,0:T(8,128)S(1)} %bitcast.286), channel_id=1, source_target_pairs={{0,4},{1,5},{2,6},{3,7},{4,0},{5,1},{6,2},{7,3},{8,12},{9,13},{10,... | collective-permute-start | bytes 1572872 | tf_op jit(solution)/shard_map/ppermute | solution.py:13
  143.2 43.6 %collective-permute-start.7 = (f32[2,256,256]{2,1,0:T(8,128)S(1)}, f32[2,256,256]{2,1,0:T(8,128)S(1)}, u32[]{:S(2)}, u32[]{:S(2)}) collective-permute-start(f32[2,256,256]{2,1,0:T(8,128)S(1)} %bitcast.294), channel_id=1, source_target_pairs={{0,4},{1,5},{2,6},{3,7},{4,0},{5,1},{6,2},{7,3},{8,12},{9,13},{10,... | collective-permute-start | bytes 1572872 | tf_op jit(solution)/shard_map/ppermute | solution.py:13
  194.2 39.1 %collective-permute-start.9 = (f32[2,256,512]{1,2,0:T(8,128)S(1)}, f32[2,256,512]{1,2,0:T(8,128)S(1)}, u32[]{:S(2)}, u32[]{:S(2)}) collective-permute-start(f32[2,256,512]{1,2,0:T(8,128)S(1)} %subtract_select_fusion.2), channel_id=1, source_target_pairs={{0,8},{1,9},{2,10},{3,11},{4,12},{5,13},{6,14},{7,15},{8,0},{9,1},... | collective-permute-start | bytes 3145736 | tf_op jit(solution)/shard_map/ppermute | solution.py:13
  198.0 35.3 %collective-permute-start.11 = (f32[2,256,256]{2,1,0:T(8,128)S(1)}, f32[2,256,256]{2,1,0:T(8,128)}, u32[]{:S(2)}, u32[]{:S(2)}) collective-permute-start(f32[2,256,256]{2,1,0:T(8,128)S(1)} %bitcast.287), channel_id=1, source_target_pairs={{0,8},{1,9},{2,10},{3,11},{4,12},{5,13},{6,14},{7,15},{8,0},{9,1},... | collective-permute-start | bytes 1572872 | tf_op jit(solution)/shard_map/ppermute | solution.py:13
  198.1 43.1 %collective-permute-start.10 = (f32[2,256,256]{2,1,0:T(8,128)S(1)}, f32[2,256,256]{2,1,0:T(8,128)}, u32[]{:S(2)}, u32[]{:S(2)}) collective-permute-start(f32[2,256,256]{2,1,0:T(8,128)S(1)} %bitcast.295), channel_id=1, source_target_pairs={{0,8},{1,9},{2,10},{3,11},{4,12},{5,13},{6,14},{7,15},{8,0},{9,1},... | collective-permute-start | bytes 1572872 | tf_op jit(solution)/shard_map/ppermute | solution.py:13
  233.4 2.7 copy-start.13
  342.7 5.2 copy-start.27
  342.7 5.2 copy-start.28
  342.7 5.3 %copy-start.25 = (s32[16,128]{1,0:T(8,128)S(1)}, s32[16,128]{1,0:T(8,128)}, u32[]{:S(2)}) copy-start(s32[16,128]{1,0:T(8,128)} %param.22) | copy-start | bytes 24580
  342.7 54.8 %all-to-all-start = ((f32[8,2,128,512]{3,2,1,0:T(8,128)}), f32[8,2,128,512]{3,2,1,0:T(8,128)}, u32[]{:S(2)}, u32[]{:S(2)}) async-start(f32[8,2,128,512]{3,2,1,0:T(8,128)} %stack.2), calls=%async_computation | async-start | bytes 8388608 | tf_op jit(solution)/shard_map/all_to_all | solution.py:83
  397.5 2.8 copy-start.11
  400.3 3.5 copy-start.24
  404.4 4.0 copy-start.5
  406.3 2.1 copy-start.6
  407.2 20.6 %collective-permute-start.12 = (f32[1,256,512]{2,1,0:T(8,128)}, f32[1,256,512]{2,1,0:T(8,128)S(1)}, u32[]{:S(2)}, u32[]{:S(2)}) collective-permute-start(f32[1,256,512]{2,1,0:T(8,128)} %slice.23), channel_id=1, source_target_pairs={{0,1},{1,0},{2,3},{3,2},{4,5},{5,4},{6,7},{7,6},{8,9},{9,8},{10,11... | collective-permute-start | bytes 1572872 | tf_op jit(solution)/shard_map/ppermute | solution.py:13
  408.4 25.2 %copy-start.7 = (f32[1,1024,512]{2,1,0:T(8,128)S(1)}, f32[1,1024,512]{2,1,0:T(8,128)}, u32[]{:S(2)}) copy-start(f32[1,1024,512]{2,1,0:T(8,128)} %copy-done.6) | copy-start | bytes 6291460
  408.4 19.4 %collective-permute-start.14 = (f32[1,256,256]{2,1,0:T(8,128)S(1)}, f32[1,256,256]{2,1,0:T(8,128)S(1)}, u32[]{:S(2)}, u32[]{:S(2)}) collective-permute-start(f32[1,256,256]{2,1,0:T(8,128)S(1)} %bitcast.288), channel_id=1, source_target_pairs={{0,1},{1,0},{2,3},{3,2},{4,5},{5,4},{6,7},{7,6},{8,9},{9,8},{10,11... | collective-permute-start | bytes 786440 | tf_op jit(solution)/shard_map/ppermute | solution.py:13
  409.2 22.8 %collective-permute-start.13 = (f32[1,256,256]{2,1,0:T(8,128)}, f32[1,256,256]{2,1,0:T(8,128)S(1)}, u32[]{:S(2)}, u32[]{:S(2)}) collective-permute-start(f32[1,256,256]{2,1,0:T(8,128)} %bitcast.12), channel_id=1, source_target_pairs={{0,1},{1,0},{2,3},{3,2},{4,5},{5,4},{6,7},{7,6},{8,9},{9,8},{10,11... | collective-permute-start | bytes 786440 | tf_op jit(solution)/shard_map/ppermute | solution.py:13
  427.8 4.2 copy-start.20
  435.3 22.1 %collective-permute-start.15 = (f32[1,256,512]{2,1,0:T(8,128)S(1)}, f32[1,256,512]{2,1,0:T(8,128)S(1)}, u32[]{:S(2)}, u32[]{:S(2)}) collective-permute-start(f32[1,256,512]{2,1,0:T(8,128)S(1)} %fusion.30), channel_id=1, source_target_pairs={{0,2},{1,3},{2,0},{3,1},{4,6},{5,7},{6,4},{7,5},{8,10},{9,11},{10,... | collective-permute-start | bytes 1572872 | tf_op jit(solution)/shard_map/ppermute | solution.py:13
  437.5 19.9 %collective-permute-start.17 = (f32[1,256,256]{2,1,0:T(8,128)S(1)}, f32[1,256,256]{2,1,0:T(8,128)}, u32[]{:S(2)}, u32[]{:S(2)}) collective-permute-start(f32[1,256,256]{2,1,0:T(8,128)S(1)} %bitcast.289), channel_id=1, source_target_pairs={{0,2},{1,3},{2,0},{3,1},{4,6},{5,7},{6,4},{7,5},{8,10},{9,11},{10,... | collective-permute-start | bytes 786440 | tf_op jit(solution)/shard_map/ppermute | solution.py:13
  439.0 21.8 %collective-permute-start.16 = (f32[1,256,256]{2,1,0:T(8,128)}, f32[1,256,256]{2,1,0:T(8,128)}, u32[]{:S(2)}, u32[]{:S(2)}) collective-permute-start(f32[1,256,256]{2,1,0:T(8,128)} %bitcast.12), channel_id=1, source_target_pairs={{0,2},{1,3},{2,0},{3,1},{4,6},{5,7},{6,4},{7,5},{8,10},{9,11},{10,... | collective-permute-start | bytes 786440 | tf_op jit(solution)/shard_map/ppermute | solution.py:13
  457.5 3.3 copy-start.17
  464.4 20.9 %collective-permute-start.18 = (f32[1,256,512]{2,1,0:T(8,128)S(1)}, f32[1,256,512]{2,1,0:T(8,128)}, u32[]{:S(2)}, u32[]{:S(2)}) collective-permute-start(f32[1,256,512]{2,1,0:T(8,128)S(1)} %fusion.28), channel_id=1, source_target_pairs={{0,4},{1,5},{2,6},{3,7},{4,0},{5,1},{6,2},{7,3},{8,12},{9,13},{10,... | collective-permute-start | bytes 1572872 | tf_op jit(solution)/shard_map/ppermute | solution.py:13
  465.6 18.9 %collective-permute-start.20 = (f32[1,256,256]{2,1,0:T(8,128)S(1)}, f32[1,256,256]{2,1,0:T(8,128)S(1)}, u32[]{:S(2)}, u32[]{:S(2)}) collective-permute-start(f32[1,256,256]{2,1,0:T(8,128)S(1)} %bitcast.290), channel_id=1, source_target_pairs={{0,4},{1,5},{2,6},{3,7},{4,0},{5,1},{6,2},{7,3},{8,12},{9,13},{10,... | collective-permute-start | bytes 786440 | tf_op jit(solution)/shard_map/ppermute | solution.py:13
  466.5 21.0 %collective-permute-start.19 = (f32[1,256,256]{2,1,0:T(8,128)}, f32[1,256,256]{2,1,0:T(8,128)}, u32[]{:S(2)}, u32[]{:S(2)}) collective-permute-start(f32[1,256,256]{2,1,0:T(8,128)} %bitcast.12), channel_id=1, source_target_pairs={{0,4},{1,5},{2,6},{3,7},{4,0},{5,1},{6,2},{7,3},{8,12},{9,13},{10,... | collective-permute-start | bytes 786440 | tf_op jit(solution)/shard_map/ppermute | solution.py:13
  485.2 4.0 copy-start.22
  487.2 9.5 %copy-start.4 = (f32[2,1024,512]{1,2,0:T(8,128)S(1)}, f32[2,1024,512]{1,2,0:T(8,128)}, u32[]{:S(2)}) copy-start(f32[2,1024,512]{1,2,0:T(8,128)} %copy-done.3) | copy-start | bytes 12582916
  491.1 20.7 %collective-permute-start.21 = (f32[1,256,512]{2,1,0:T(8,128)S(1)}, f32[1,256,512]{2,1,0:T(8,128)S(1)}, u32[]{:S(2)}, u32[]{:S(2)}) collective-permute-start(f32[1,256,512]{2,1,0:T(8,128)S(1)} %fusion.26), channel_id=1, source_target_pairs={{0,8},{1,9},{2,10},{3,11},{4,12},{5,13},{6,14},{7,15},{8,0},{9,1},... | collective-permute-start | bytes 1572872 | tf_op jit(solution)/shard_map/ppermute | solution.py:13
  493.2 18.5 %collective-permute-start.23 = (f32[1,256,256]{2,1,0:T(8,128)S(1)}, f32[1,256,256]{2,1,0:T(8,128)}, u32[]{:S(2)}, u32[]{:S(2)}) collective-permute-start(f32[1,256,256]{2,1,0:T(8,128)S(1)} %bitcast.291), channel_id=1, source_target_pairs={{0,8},{1,9},{2,10},{3,11},{4,12},{5,13},{6,14},{7,15},{8,0},{9,1},... | collective-permute-start | bytes 786440 | tf_op jit(solution)/shard_map/ppermute | solution.py:13
  494.7 19.9 %collective-permute-start.22 = (f32[1,256,256]{2,1,0:T(8,128)}, f32[1,256,256]{2,1,0:T(8,128)}, u32[]{:S(2)}, u32[]{:S(2)}) collective-permute-start(f32[1,256,256]{2,1,0:T(8,128)} %bitcast.12), channel_id=1, source_target_pairs={{0,8},{1,9},{2,10},{3,11},{4,12},{5,13},{6,14},{7,15},{8,0},{9,1},... | collective-permute-start | bytes 786440 | tf_op jit(solution)/shard_map/ppermute | solution.py:13
  513.4 4.7 slice-start
  516.2 3.4 copy-start.1
  (8 other events, 9.3 us)
Sparse Core Ops, SparseCore 0:
  251.3 87.5 all-reduce.1
